TPU v7x, 128 devices: a whole 4x4x4 slice. The times are simulated.
128 devices in a mesh: facet: 8 (over y, core), sub: 16 (over x, z).
Axes of the slice: x: 4, y: 4, z: 4, core: 2. Of those that a mesh axis runs over, the one named last changes fastest.
Arguments:
- facets: bfloat16 [8, 1024, 1024], P('facet'), may hold values from -6 to 6
- tapers: float32 [2, 1024], replicated, may hold values from 0.2 to 1
- row_offsets: int32 [8], replicated, may hold values from 0 to 7679
- col_offsets: int32 [16], P('sub'), may hold values from 0 to 7679
- block_subgrid: int32 [128, 1], P(('facet', 'sub')), may hold values from 0 to 15; in each aligned block of 16 rows (0 to 15, 16 to 31, ...) at most 2 rows name the same one
- vis_count: int32 [128], P(('facet', 'sub')), may hold values from 1 to 1024, 81920 in all
- positions: float32 [128, 2, 1024], P(('facet', 'sub')), may hold values from -0.5 to 0.5
- observed: float32 [128, 2, 1024], P(('facet', 'sub')), may hold values from -6 to 6
Outputs:
- residual_vis: float32 [128, 2, 1024], P(('facet', 'sub'))
- residual_subgrids: float32 [8, 16, 512, 1024], P('facet', 'sub')
Inputs may be any that keep to these rules, and one draw needn't show every extreme that they name: `block_subgrid`: among the blocks of one index of facet (aligned blocks of 16 rows), at most 2 name the same column, and in every draw some column is named by exactly 2 of them. `vis_count`: the largest count over all blocks is exactly 1024.
All inputs are finite; a program needn't handle non-finite values.
Results may differ from a plain program's by a relative error of at most 0.013.
Values may be sent and summed in bfloat16 or wider, within the bound.
A program may use at most 64 MiB of HBM per device.

v0:
```python
import functools
import math

import jax
import jax.numpy as jnp
from jax import lax
from jax.experimental import pallas as pl
from jax.experimental.pallas import tpu as pltpu
from jax.sharding import PartitionSpec as P

M = 512
HALF = 256
FS = 1024
NIMG = 8192
ROWS = 1024
NF = 8
NS = 16
MESH = pl.DeviceIdType.MESH
F32 = jnp.float32
BF16 = jnp.bfloat16
I32 = jnp.int32


def turn(t):
    u = (t - jnp.round(t)) * math.pi
    v = u * u
    s = 1.0 / 6227020800.0
    for c in (-1.0 / 39916800.0, 1.0 / 362880.0, -1.0 / 5040.0, 1.0 / 120.0, -1.0 / 6.0, 1.0):
        s = s * v + c
    s = s * u
    k = 1.0 / 479001600.0
    for c in (-1.0 / 3628800.0, 1.0 / 40320.0, -1.0 / 720.0, 1.0 / 24.0, -0.5, 1.0):
        k = k * v + c
    return 1.0 - 2.0 * s * s, 2.0 * s * k


def grow(base, coarse, steps, put):
    bc, bs = base

    def step(q, carry):
        cc, cs = coarse(q)
        put(q, bc * cc - bs * cs, bs * cc + bc * cs)
        return carry

    lax.fori_loop(0, steps, step, 0)


def iota(shape, dim):
    return lax.broadcasted_iota(I32, shape, dim)


def half_steps(p, n, m_ref):
    shape = (16, n)
    rows = iota(shape, 0).astype(F32)
    m_ref[0], m_ref[1] = turn(p * (rows + 0.5))
    m_ref[2], m_ref[3] = turn(p * (rows * 16.0))


def basis_into(m_ref, lanes, put):
    for at, width in lanes:
        base = (m_ref[0, :, pl.ds(at, width)], m_ref[1, :, pl.ds(at, width)])

        def coarse(q, at=at, width=width):
            return m_ref[2, pl.ds(q, 1), pl.ds(at, width)], m_ref[3, pl.ds(q, 1), pl.ds(at, width)]

        def put_here(q, c, s, at=at, width=width):
            put(pl.multiple_of(q * 16, 16), at, width, c, s)

        grow(base, coarse, 16, put_here)


def front(
    facets, tapers, row_off, col_off, target, count, pos, obs,
    res_out, grid_out,
    res_all, pos_all, meta_all, fac, tt, facs, bt, zs, ptn, qg, qm, ec, es, ub, vb, hs, hacc, small, meta_src,
    mask, slot_pos, ubo, vbo, wb, total,
    load_sem, a_send, a_recv, d_send, d_recv, b_send, b_recv, m_send, m_recv, p_send, p_recv, c_send, c_recv,
):
    f = lax.axis_index("facet")
    j = lax.axis_index("sub")
    core = lax.rem(f, 2)
    x, z = j // 4, lax.rem(j, 4)
    pair, odd = j // 2, lax.rem(j, 2)
    at128 = pl.multiple_of(pair * 128, 128)

    load = pltpu.make_async_copy(facets.at[0, :, pl.ds(at128, 128)], fac, load_sem)
    load.start()

    barrier = pltpu.get_barrier_semaphore()
    for d in range(1, NF):
        pl.semaphore_signal(barrier, inc=1, device_id={"facet": lax.rem(f + d, NF)}, device_id_type=MESH)
    for d in range(1, NS):
        pl.semaphore_signal(barrier, inc=1, device_id={"sub": lax.rem(j + d, NS)}, device_id_type=MESH)

    rows8 = iota((8, 128), 0)
    meta_src[...] = jnp.where(rows8 == 0, col_off[0], jnp.where(rows8 == 1, target[0, 0], count[0]))
    meta_all[j] = meta_src[...]
    pos_all[j] = pos[0]

    load.wait()
    by_column = fac[...].astype(F32) * tapers[1:2, pl.ds(at128, 128)]
    turned = (by_column.T * tapers[0:1, :]).astype(BF16)
    for g in range(4):
        tt[g] = turned[g * 32 : g * 32 + 32]
    facs[f] = tt[2 * odd + core]

    pl.semaphore_wait(barrier, NF - 1 + NS - 1)
    a_copies, m_copies = [], []
    for d in range(1, NF):
        peer = lax.rem(f + d, NF)
        copy = pltpu.make_async_remote_copy(
            src_ref=tt.at[2 * odd + lax.rem(peer, 2)], dst_ref=facs.at[f],
            send_sem=a_send.at[d - 1], recv_sem=a_recv.at[d - 1],
            device_id={"facet": peer}, device_id_type=MESH,
        )
        copy.start()
        a_copies.append(copy)
    for d in range(1, NS):
        peer = lax.rem(j + d, NS)
        for src, dst, ss, rs in ((meta_src, meta_all, m_send, m_recv), (pos.at[0], pos_all, p_send, p_recv)):
            copy = pltpu.make_async_remote_copy(
                src_ref=src, dst_ref=dst.at[j], send_sem=ss.at[d - 1], recv_sem=rs.at[d - 1],
                device_id={"sub": peer}, device_id_type=MESH,
            )
            copy.start()
            m_copies.append(copy)

    lanes4 = [(0, 256), (256, 256), (512, 256), (768, 256)]

    def table_into(ref, lead, dtype):
        def put(at, lane_at, width, c, s):
            ref[(*lead, pl.ds(at, 16), pl.ds(lane_at, width))] = c.astype(dtype)
            ref[(*lead, pl.ds(at + HALF, 16), pl.ds(lane_at, width))] = s.astype(dtype)

        basis_into(small, lanes4, put)

    lane = iota((16, FS), 1)
    row = iota((16, FS), 0)
    crossed = ((lane >> 6) & 3) * 256 + (lane >> 8) * 64 + (lane & 63)
    for order, at in enumerate((lane, crossed)):
        small[0], small[1] = turn((((2 * row + 1) * at) & 2047).astype(F32) * (1.0 / 2048))
        small[2], small[3] = turn(((32 * row * at) & 2047).astype(F32) * (1.0 / 2048))
        table_into(bt, (order,), BF16)
    half_steps(pos[0, 0:1, :], FS, small)
    table_into(ub, (), BF16)
    half_steps(pos[0, 1:2, :], FS, small)
    table_into(vb, (), F32)

    phases = []
    rows_f = iota((NF, FS), 0)
    lane_f = iota((NF, FS), 1)
    for aa in range(2):
        off = row_off[2 * (f // 2) + aa]
        r = (off * (rows_f * FS + lane_f) + 2044 * lane_f) & (NIMG - 1)
        c, s = turn(r.astype(F32) * (1.0 / NIMG))
        phases.append((c, -s))

    for d in range(1, NF):
        a_copies[d - 1].wait_recv()
    for at, width in lanes4:
        sums = [jnp.zeros((32, width), F32) for _ in range(4)]
        for g in range(NF):
            t = facs[g, :, at : at + width].astype(F32)
            for aa in range(2):
                sums[2 * aa] = sums[2 * aa] + t * phases[aa][0][g : g + 1, at : at + width]
                sums[2 * aa + 1] = sums[2 * aa + 1] + t * phases[aa][1][g : g + 1, at : at + width]
        for i in range(4):
            zs[i * 32 : i * 32 + 32, at : at + width] = sums[i].astype(BF16)
    turned_rows = lax.dot_general(
        zs[...], bt[0], (((1,), (1,)), ((), ())), preferred_element_type=F32
    ).astype(BF16)
    q_rows = [[jnp.concatenate([
        turned_rows[aa * 64 : aa * 64 + 32, hf * HALF : hf * HALF + HALF],
        turned_rows[aa * 64 + 32 : aa * 64 + 64, hf * HALF : hf * HALF + HALF],
    ], axis=1) for hf in range(2)] for aa in range(2)]
    mine_first = core == 0
    for hf in range(2):
        qg[hf, j, core] = jnp.where(mine_first, q_rows[0][hf], q_rows[1][hf])
        ptn[hf] = jnp.where(mine_first, q_rows[1][hf], q_rows[0][hf])
    d_copies = []
    for hf in range(2):
        copy = pltpu.make_async_remote_copy(
            src_ref=ptn.at[hf], dst_ref=qg.at[hf, j, core],
            send_sem=d_send.at[hf], recv_sem=d_recv.at[hf],
            device_id={"facet": f + 1 - 2 * core}, device_id_type=MESH,
        )
        copy.start()
        d_copies.append(copy)

    def place(hf, dp, dq):
        dx, dz = (dq, dp) if hf == 0 else (dp, dq)
        return 4 * lax.rem(x + dx % 4, 4) + lax.rem(z + dz % 4, 4)

    b_copies = []

    def send(hf, dp, dq, rh, ep, eq):
        copy = pltpu.make_async_remote_copy(
            src_ref=qg.at[hf, place(hf, dp, dq), rh], dst_ref=qg.at[hf, place(hf, dp, dq), rh],
            send_sem=b_send.at[len(b_copies)],
            recv_sem=b_recv.at[hf, (dq - eq) % 4, (dp - ep) % 4, rh],
            device_id={"sub": place(hf, ep, eq)}, device_id_type=MESH,
        )
        copy.start()
        b_copies.append(copy)

    def arrived(hf, dp, dq, rh):
        pltpu.make_async_remote_copy(
            src_ref=qg.at[hf, place(hf, dp, dq), rh], dst_ref=qg.at[hf, place(hf, dp, dq), rh],
            send_sem=b_send.at[0], recv_sem=b_recv.at[hf, dq % 4, dp % 4, rh],
            device_id={"sub": j}, device_id_type=MESH,
        ).wait_recv()

    four = ((0, 1), (0, -1), (1, 0), (-1, 0))
    for hf in range(2):
        for ep, eq in four:
            send(hf, 0, 0, core, ep, eq)
    for hf in range(2):
        pltpu.make_async_remote_copy(
            src_ref=ptn.at[hf], dst_ref=qg.at[hf, j, 1 - core],
            send_sem=d_send.at[hf], recv_sem=d_recv.at[hf],
            device_id={"facet": f + 1 - 2 * core}, device_id_type=MESH,
        ).wait_recv()
        for ep, eq in four:
            send(hf, 0, 0, 1 - core, ep, eq)

    for copy in m_copies:
        copy.wait_recv()
    step = meta_all[target[0, 0]][0:1, :] + 2044
    rows128 = iota((16, 128), 0)
    base_c, base_s = turn(((step * rows128) & (NIMG - 1)).astype(F32) * (1.0 / NIMG))
    for part in range(4):
        coarse_c, coarse_s = turn(((step * (16 * (iota((16, 128), 0) + 16 * part))) & (NIMG - 1)).astype(F32) * (1.0 / NIMG))
        for q in range(16):
            cc, cs = coarse_c[q : q + 1], coarse_s[q : q + 1]
            at = part * 256 + q * 16
            ec[at : at + 16] = base_c * cc - base_s * cs
            es[at : at + 16] = -(base_s * cc + base_c * cs)

    for dp in (-1, 1):
        for rh in range(2):
            for hf in range(2):
                arrived(hf, dp, 0, rh)
                send(hf, dp, 0, rh, 0, 1)
                send(hf, dp, 0, rh, 0, -1)
                if rh == (0 if dp == -1 else 1):
                    send(hf, dp, 0, rh, -dp, 0)

    rank = jnp.zeros((1, 128), F32)
    slots = [jnp.zeros((2, ROWS), F32) for _ in range(2)]
    for b in range(NS):
        match = jnp.where(meta_all[b, 1:2, :] == j, 1.0, 0.0)
        for slot in range(2):
            picked = jnp.where(rank == float(slot), match, 0.0)
            mask[slot, b : b + 1, :] = picked
            slots[slot] = slots[slot] + picked[:, 0:1] * pos_all[b]
        rank = rank + match
    for slot in range(2):
        slot_pos[slot] = slots[slot]

    def slot_table(slot, k):
        half_steps(slot_pos[slot, k : k + 1, :], ROWS, small)
        if k == 0:
            table_into(ubo, (slot,), BF16)
        else:
            table_into(vbo, (slot,), F32)

    def across(dp):
        for dq in (-1, 1):
            for rh in range(2):
                for hf in range(2):
                    arrived(hf, dp, dq, rh)
                    if rh == (0 if dq == -1 else 1):
                        send(hf, dp, dq, rh, 0, -dq)

    def transform(dq):
        for hf in range(2):
            line = lax.rem((x if hf == 0 else z) + dq % 4, 4)

            def modulate(i, carry, hf=hf, line=line):
                k4, rh = i // 2, lax.rem(i, 2)
                src = 4 * line + k4 if hf == 0 else 4 * k4 + line
                at = pl.multiple_of(src * 64 + rh * 32, 32)
                to = pl.multiple_of(i * 32, 32)
                c, s = ec[pl.ds(at, 32)], es[pl.ds(at, 32)]
                for k in range(2):
                    re = qg[hf, src, rh, :, k * 128 : k * 128 + 128].astype(F32)
                    im = qg[hf, src, rh, :, 256 + k * 128 : 384 + k * 128].astype(F32)
                    qm[hf, pl.ds(to, 32), k * 128 : k * 128 + 128] = (re * c - im * s).astype(BF16)
                    qm[hf, pl.ds(to, 32), 256 + k * 128 : 384 + k * 128] = (re * s + im * c).astype(BF16)
                return carry

            lax.fori_loop(0, 8, modulate, 0)
        for hf in range(2):
            line = lax.rem((x if hf == 0 else z) + dq % 4, 4)
            part = jnp.dot(
                bt[hf, :, pl.ds(pl.multiple_of(line * 256, 256), 256)], qm[hf], preferred_element_type=F32
            )
            if dq == 0:
                hacc[hf] = part
            elif dq == 2:
                both = (hacc[hf] + part).astype(BF16)
                hs[0:M, hf * HALF : hf * HALF + HALF] = both[:, 0:HALF]
                hs[M : 2 * M, hf * HALF : hf * HALF + HALF] = both[:, HALF:M]
            else:
                hacc[hf] += part

    across(0)
    slot_table(0, 0)
    for rh in range(2):
        for hf in range(2):
            arrived(hf, 2, 0, rh)
            send(hf, 2, 0, rh, 0, 1)
            send(hf, 2, 0, rh, 0, -1)
    slot_table(0, 1)
    across(-1)
    across(1)
    transform(0)
    slot_table(1, 0)
    across(2)
    slot_table(1, 1)
    transform(-1)
    transform(1)
    for dp in (0, -1, 1, 2):
        for rh in range(2):
            for hf in range(2):
                arrived(hf, dp, 2, rh)
    transform(2)

    live_count = count[0]

    for at in range(0, ROWS, 256):
        lifted = jnp.dot(hs[...], ub[:, pl.ds(at, 256)], preferred_element_type=F32)
        v = vb[:, pl.ds(at, 256)]
        sum_re = jnp.sum(lifted[0:M] * v, axis=0, keepdims=True)
        sum_im = jnp.sum(lifted[M : 2 * M] * v, axis=0, keepdims=True)
        c, s = turn((pos[0, 0:1, pl.ds(at, 256)] + pos[0, 1:2, pl.ds(at, 256)]) * 0.5)
        scale = 4.0 / (M * FS)
        live = iota((1, 256), 1) + at < live_count
        re = obs[0, 0:1, pl.ds(at, 256)] - (sum_re * c + sum_im * s) * scale
        im = obs[0, 1:2, pl.ds(at, 256)] - (sum_im * c - sum_re * s) * scale
        res_out[0, 0:1, pl.ds(at, 256)] = jnp.where(live, re, 0.0)
        res_out[0, 1:2, pl.ds(at, 256)] = jnp.where(live, im, 0.0)

    c_copies = []
    for d in range(1, NS):
        copy = pltpu.make_async_remote_copy(
            src_ref=res_out.at[0], dst_ref=res_all.at[j], send_sem=c_send.at[d - 1], recv_sem=c_recv.at[d - 1],
            device_id={"sub": lax.rem(j + d, NS)}, device_id_type=MESH,
        )
        copy.start()
        c_copies.append(copy)
    res_all[j] = res_out[0]
    for copy in a_copies + m_copies + d_copies + b_copies:
        copy.wait_send()
    for copy in c_copies:
        copy.wait()

    rows = []
    for slot in range(2):
        r = jnp.zeros((2, ROWS), F32)
        for b in range(NS):
            r = r + mask[slot, b : b + 1, 0:1] * res_all[b]
        p = slot_pos[slot]
        c, s = turn((p[0:1, :] + p[1:2, :]) * 0.5)
        rows.append((r[0:1, :] * c - r[1:2, :] * s, r[0:1, :] * s + r[1:2, :] * c))
    for block in range(4):
        im, sine = block // 2, block % 2
        for slot in range(2):
            wb[block, :, slot * ROWS : slot * ROWS + ROWS] = (
                vbo[slot, sine * HALF : sine * HALF + HALF, :] * rows[slot][im]
            ).astype(BF16)
        for k in range(2):
            total[k, block] = sum(
                lax.dot_general(
                    ubo[slot, k * HALF : k * HALF + HALF, :], wb[block, :, slot * ROWS : slot * ROWS + ROWS],
                    (((1,), (1,)), ((), ())), preferred_element_type=F32,
                )
                for slot in range(2)
            )

    scale = 1.0 / math.sqrt(ROWS)
    flip = jnp.where(iota((HALF, HALF), 0) + iota((HALF, HALF), 1) == HALF - 1, 1.0, 0.0).astype(BF16)

    def flip_columns(a):
        return jnp.dot(a.astype(BF16), flip, preferred_element_type=F32).astype(BF16)

    def flip_rows(a):
        return jnp.dot(flip, a, preferred_element_type=F32).astype(BF16)

    for im in range(2):
        sign = 1.0 if im == 0 else -1.0
        cc, ss = total[0, 2 * im], total[1, 2 * im + 1]
        cs, sc = total[0, 3 - 2 * im], total[1, 2 - 2 * im]
        even, both = (cc - ss) * scale, (cc + ss) * scale
        y, w = (cs + sc) * (scale * sign), (cs - sc) * (scale * sign)
        left, right = slice(im * M, im * M + HALF), slice(im * M + HALF, im * M + M)
        grid_out[0, 0, HALF:M, right] = (even + y).astype(BF16)
        grid_out[0, 0, HALF:M, left] = flip_columns(both - w)
        grid_out[0, 0, 0:HALF, right] = flip_rows((both + w).astype(BF16))
        grid_out[0, 0, 0:HALF, left] = flip_rows(flip_columns(even - y))


def per_device(facets, tapers, row_offsets, col_offsets, block_subgrid, vis_count, positions, observed):
    vmem = pl.BlockSpec(memory_space=pltpu.VMEM)
    smem = pl.BlockSpec(memory_space=pltpu.SMEM)
    dma = pltpu.SemaphoreType.DMA
    residual, grid = pl.pallas_call(
        front,
        out_shape=(
            jax.ShapeDtypeStruct((1, 2, ROWS), F32),
            jax.ShapeDtypeStruct((1, 1, M, 2 * M), BF16),
        ),
        in_specs=[pl.BlockSpec(memory_space=pl.ANY), vmem, smem, smem, smem, smem, vmem, vmem],
        out_specs=(vmem, vmem),
        scratch_shapes=[
            pltpu.VMEM((NS, 2, ROWS), F32),
            pltpu.VMEM((NS, 2, ROWS), F32),
            pltpu.VMEM((NS, 8, 128), I32),
            pltpu.VMEM((FS, 128), BF16),
            pltpu.VMEM((4, 32, FS), BF16),
            pltpu.VMEM((NF, 32, FS), BF16),
            pltpu.VMEM((2, M, FS), BF16),
            pltpu.VMEM((128, FS), BF16),
            pltpu.VMEM((2, 32, M), BF16),
            pltpu.VMEM((2, NS, 2, 32, M), BF16),
            pltpu.VMEM((2, 256, M), BF16),
            pltpu.VMEM((FS, 128), F32),
            pltpu.VMEM((FS, 128), F32),
            pltpu.VMEM((M, ROWS), BF16),
            pltpu.VMEM((M, ROWS), F32),
            pltpu.VMEM((2 * M, M), BF16),
            pltpu.VMEM((2, M, M), F32),
            pltpu.VMEM((4, 16, FS), F32),
            pltpu.VMEM((8, 128), I32),
            pltpu.VMEM((2, NS, 128), F32),
            pltpu.VMEM((2, 2, ROWS), F32),
            pltpu.VMEM((2, M, ROWS), BF16),
            pltpu.VMEM((2, M, ROWS), F32),
            pltpu.VMEM((4, HALF, 2 * ROWS), BF16),
            pltpu.VMEM((2, 4, HALF, HALF), F32),
            dma(()),
            dma((NF - 1,)), dma((NF - 1,)),
            dma((2,)), dma((2,)),
            dma((60,)), dma((2, 4, 4, 2)),
            dma((NS - 1,)), dma((NS - 1,)),
            dma((NS - 1,)), dma((NS - 1,)),
            dma((NS - 1,)), dma((NS - 1,)),
        ],
        compiler_params=pltpu.CompilerParams(collective_id=0, has_side_effects=True),
        name="front",
    )(facets, tapers, row_offsets, col_offsets, block_subgrid, vis_count, positions, observed)
    return residual, grid.astype(F32)


def solution(mesh):
    in_specs = (
        P("facet", None, None),
        P(),
        P(),
        P("sub"),
        P(("facet", "sub"), None),
        P(("facet", "sub")),
        P(("facet", "sub"), None, None),
        P(("facet", "sub"), None, None),
    )
    out_specs = (P(("facet", "sub"), None, None), P("facet", "sub", None, None))
    return jax.shard_map(per_device, mesh=mesh, in_specs=in_specs, out_specs=out_specs, check_vma=False)
```

profile of v0, /device:TPU:0, one launch (start us, length us, event | category | flops | bytes accessed | tf_op | source)
XLA Modules:
  0.0 53.1 jit_solution(18226258346975543770)
XLA Ops:
  2.6 47.2 %front.1 = (f32[1,2,1024]{2,1,0:T(2,128)}, bf16[1,1,512,1024]{3,2,1,0:T(8,128)(2,1)}) custom-call(bf16[1,1024,1024]{2,1,0:T(8,128)(2,1)} %facets.1, f32[2,1024]{1,0:T(2,128)} %tapers.1, s32[8]{0:T(128)} %row_off.1, s32[1]{0:T(128)S(6)} %copy.11.col_off, s32[1,1]{1,0:T(1,128)S(6)} %copy.12.target, s32[1]{0:T(128)S(6)} %copy.13.count, f32[1,2,1024]{2,1,0:T(2,128)} %pos.1, ...), custom_call_target="tpu_custom_call" | custom-call | tf_op jit(solution)/shard_map/front/pallas_call | solution.py:407
  49.7 0.0 copy-start
  49.7 2.8 %convert_element_type.3 = f32[1,1,512,1024]{3,2,1,0:T(8,128)} convert(bf16[1,1,512,1024]{3,2,1,0:T(8,128)(2,1)} %get-tuple-element.5) | non-fusion elementwise | flops 524288 | bytes 3145728 | tf_op jit(solution)/shard_map/convert_element_type | solution.py:452
  52.5 0.0 copy-done
  52.5 0.6 %copy.14 = f32[1,2,1024]{2,1,0:T(2,128)} copy(f32[1,2,1024]{2,1,0:T(2,128)S(1)} %copy-done) | data formatting | bytes 16384
Async XLA Ops:
  49.7 2.8 %copy-start = (f32[1,2,1024]{2,1,0:T(2,128)S(1)}, f32[1,2,1024]{2,1,0:T(2,128)}, u32[]{:S(2)}) copy-start(f32[1,2,1024]{2,1,0:T(2,128)} %get-tuple-element.8) | copy-start | bytes 24580
where the time goes:
time: 53.4 us; the launch traced here: 53.1 us
  Pallas kernels  47.2 us (88%)
  other arithmetic  2.79 us (5%)
  between operations  2.58 us (5%)
  local copies, waits for them, and re-layouts  0.6 us (1%)
    pallas_call x1, Pallas kernels, per_device(): pl.pallas_call(front, out_shape=(jax.ShapeDtypeStruct((1, 2, ROWS), F32),...  47.2 us
    convert_element_type x1, other arithmetic, per_device(): return (residual, grid.astype(F32))  2.79 us

commit v1 on v0

v1 whole, which is shorter than its diff:
```python
import functools
import math

import jax
import jax.numpy as jnp
from jax import lax
from jax.experimental import pallas as pl
from jax.experimental.pallas import tpu as pltpu
from jax.sharding import PartitionSpec as P

M = 512
HALF = 256
FS = 1024
NIMG = 8192
ROWS = 1024
NF = 8
NS = 16
MESH = pl.DeviceIdType.MESH
F32 = jnp.float32
BF16 = jnp.bfloat16
I32 = jnp.int32


def turn(t):
    u = (t - jnp.round(t)) * math.pi
    v = u * u
    s = 1.0 / 6227020800.0
    for c in (-1.0 / 39916800.0, 1.0 / 362880.0, -1.0 / 5040.0, 1.0 / 120.0, -1.0 / 6.0, 1.0):
        s = s * v + c
    s = s * u
    k = 1.0 / 479001600.0
    for c in (-1.0 / 3628800.0, 1.0 / 40320.0, -1.0 / 720.0, 1.0 / 24.0, -0.5, 1.0):
        k = k * v + c
    return 1.0 - 2.0 * s * s, 2.0 * s * k


def grow(base, coarse, steps, put):
    bc, bs = base

    def step(q, carry):
        cc, cs = coarse(q)
        put(q, bc * cc - bs * cs, bs * cc + bc * cs)
        return carry

    lax.fori_loop(0, steps, step, 0)


def iota(shape, dim):
    return lax.broadcasted_iota(I32, shape, dim)


def half_steps(p, n, m_ref, start=0.0):
    shape = (16, n)
    rows = iota(shape, 0).astype(F32)
    m_ref[0], m_ref[1] = turn(p * (rows + 0.5))
    m_ref[2], m_ref[3] = turn(p * (rows * 16.0 + start))


def basis_into(m_ref, lanes, put, steps=16):
    for at, width in lanes:
        base = (m_ref[0, :, pl.ds(at, width)], m_ref[1, :, pl.ds(at, width)])

        def coarse(q, at=at, width=width):
            return m_ref[2, pl.ds(q, 1), pl.ds(at, width)], m_ref[3, pl.ds(q, 1), pl.ds(at, width)]

        def put_here(q, c, s, at=at, width=width):
            put(pl.multiple_of(q * 16, 16), at, width, c, s)

        grow(base, coarse, steps, put_here)


def front(
    facets, taper_in, row_off_in, col_off_in, target_in, count_in, pos_in, obs_in,
    res_out, grid_out,
    tapers, pos, obs, row_off, col_off, target, count, res_src,
    res_all, pos_all, meta_all, fac, tt, facs, bt, zs, uq, qg, qm, ec, es, ub, vb, hs, hacc, small, meta_src,
    mask, slot_pos, ubo, vbo, wb, total, part_out, part_in,
    load_sem, a_send, a_recv, d_send, d_recv, b_send, b_recv, m_send, m_recv, p_send, p_recv, c_send, c_recv,
):
    f = lax.axis_index("facet")
    j = lax.axis_index("sub")
    core = lax.rem(f, 2)
    x, z = j // 4, lax.rem(j, 4)
    pair, odd = j // 2, lax.rem(j, 2)
    at128 = pl.multiple_of(pair * 128, 128)

    y = f // 2
    barrier = pltpu.get_barrier_semaphore()
    near = [2 * lax.rem(y + dy, 4) + c for dy in (1, 3) for c in range(2)] + [f + 1 - 2 * core]
    for peer in near:
        pl.semaphore_signal(barrier, inc=1, device_id={"facet": peer}, device_id_type=MESH)
    for d in range(1, NS):
        pl.semaphore_signal(barrier, inc=1, device_id={"sub": lax.rem(j + d, NS)}, device_id_type=MESH)
    for dz in range(1, 4):
        other = {"facet": f + 1 - 2 * core, "sub": 4 * x + lax.rem(z + dz, 4)}
        pl.semaphore_signal(barrier, inc=1, device_id=other, device_id_type=MESH)
    loads = [
        pltpu.make_async_copy(src, dst, load_sem.at[i])
        for i, (src, dst) in enumerate((
            (facets.at[0, :, pl.ds(at128, 128)], fac), (taper_in, tapers), (pos_in, pos), (obs_in, obs),
            (row_off_in, row_off), (col_off_in, col_off), (target_in, target), (count_in, count),
        ))
    ]
    for load in loads:
        load.start()
    for load in loads:
        load.wait()

    rows8 = iota((8, 128), 0)
    meta_src[...] = jnp.where(rows8 == 0, col_off[0], jnp.where(rows8 == 1, target[0, 0], count[0]))
    meta_all[j] = meta_src[...]
    pos_all[j] = pos[0]

    by_column = fac[...].astype(F32) * tapers[1:2, pl.ds(at128, 128)]
    turned = (by_column.T * tapers[0:1, :]).astype(BF16)
    for g in range(4):
        tt[g] = turned[g * 32 : g * 32 + 32]
    facs[f] = tt[2 * odd + core]

    pl.semaphore_wait(barrier, 5 + NS - 1 + 3)
    a_copies, m_copies = [], []

    def facet_at(dy, c):
        return 2 * lax.rem(y + dy % 4, 4) + c

    def send_slice(src, source, dy, c, slot):
        copy = pltpu.make_async_remote_copy(
            src_ref=src, dst_ref=facs.at[source], send_sem=a_send.at[len(a_copies)], recv_sem=a_recv.at[slot],
            device_id={"facet": facet_at(dy, c)}, device_id_type=MESH,
        )
        copy.start()
        a_copies.append(copy)

    def slice_arrived(dy, c, slot):
        pltpu.make_async_remote_copy(
            src_ref=facs.at[facet_at(dy, c)], dst_ref=facs.at[facet_at(dy, c)],
            send_sem=a_send.at[0], recv_sem=a_recv.at[slot], device_id={"facet": f}, device_id_type=MESH,
        ).wait_recv()

    for dy in (1, 3):
        for c in range(2):
            send_slice(tt.at[2 * odd + c], f, dy, c, 2 * (4 - dy) + core)
    send_slice(tt.at[2 * odd + 1 - core], f, 0, 1 - core, 0)
    for d in range(1, NS):
        peer = lax.rem(j + d, NS)
        for src, dst, ss, rs in ((meta_src, meta_all, m_send, m_recv), (pos.at[0], pos_all, p_send, p_recv)):
            copy = pltpu.make_async_remote_copy(
                src_ref=src, dst_ref=dst.at[j], send_sem=ss.at[d - 1], recv_sem=rs.at[d - 1],
                device_id={"sub": peer}, device_id_type=MESH,
            )
            copy.start()
            m_copies.append(copy)

    lanes4 = [(0, 256), (256, 256), (512, 256), (768, 256)]

    def table_into(ref, lead, dtype):
        def put(at, lane_at, width, c, s):
            ref[(*lead, pl.ds(at, 16), pl.ds(lane_at, width))] = c.astype(dtype)
            ref[(*lead, pl.ds(at + HALF, 16), pl.ds(lane_at, width))] = s.astype(dtype)

        basis_into(small, lanes4, put)

    def relay_slices():
        slice_arrived(3, 0, 6)
        send_slice(facs.at[facet_at(3, 0)], facet_at(3, 0), 1, core, 4)
        slice_arrived(1, 1, 3)
        send_slice(facs.at[facet_at(1, 1)], facet_at(1, 1), 3, core, 5)

    lane = iota((16, FS), 1)
    row = iota((16, FS), 0)
    small[0], small[1] = turn((((2 * row + 1) * lane) & 2047).astype(F32) * (1.0 / 2048))
    small[2], small[3] = turn(((32 * row * lane) & 2047).astype(F32) * (1.0 / 2048))
    table_into(bt, (), BF16)
    relay_slices()

    phases = []
    rows_f = iota((NF, FS), 0)
    lane_f = iota((NF, FS), 1)
    for aa in range(2):
        off = row_off[2 * (f // 2) + aa]
        r = (off * (rows_f * FS + lane_f) + 2044 * lane_f) & (NIMG - 1)
        c, s = turn(r.astype(F32) * (1.0 / NIMG))
        phases.append((c, -s))

    slice_arrived(0, 1 - core, 0)
    slice_arrived(3, 1, 7)
    slice_arrived(1, 0, 2)
    slice_arrived(2, 0, 4)
    slice_arrived(2, 1, 5)
    for at, width in lanes4:
        sums = [jnp.zeros((32, width), F32) for _ in range(4)]
        for g in range(NF):
            t = facs[g, :, at : at + width].astype(F32)
            for aa in range(2):
                sums[2 * aa] = sums[2 * aa] + t * phases[aa][0][g : g + 1, at : at + width]
                sums[2 * aa + 1] = sums[2 * aa + 1] + t * phases[aa][1][g : g + 1, at : at + width]
        for i in range(4):
            zs[i * 32 : i * 32 + 32, at : at + width] = sums[i].astype(BF16)
    turned_rows = lax.dot_general(
        zs[...], bt[...], (((1,), (1,)), ((), ())), preferred_element_type=F32
    ).astype(BF16)
    for aa in range(2):
        for k in range(4):
            uq[aa, k] = jnp.concatenate([
                turned_rows[aa * 64 : aa * 64 + 32, k * 128 : k * 128 + 128],
                turned_rows[aa * 64 + 32 : aa * 64 + 64, k * 128 : k * 128 + 128],
            ], axis=1)
    qg[j, core] = uq[core, z]

    def place(dx, dz):
        return 4 * lax.rem(x + dx % 4, 4) + lax.rem(z + dz % 4, 4)

    def core_of(e):
        return core if e == 0 else 1 - core

    b_copies = []

    def send_unit(src, dst, slot, device):
        copy = pltpu.make_async_remote_copy(
            src_ref=src, dst_ref=dst, send_sem=b_send.at[len(b_copies)], recv_sem=b_recv.at[slot],
            device_id=device, device_id_type=MESH,
        )
        copy.start()
        b_copies.append(copy)

    def slot_of(dx, dz, e):
        return ((dx % 4) * 4 + dz % 4) * 2 + e

    def unit(dx, dz, e):
        return qg.at[place(dx, dz), core_of(e)]

    def along_x(dx, dz, e, ex):
        send_unit(unit(dx, dz, e), unit(dx, dz, e), slot_of(dx - ex, dz, e), {"sub": place(ex, 0)})

    def arrived(dx, dz, e):
        pltpu.make_async_remote_copy(
            src_ref=unit(dx, dz, e), dst_ref=unit(dx, dz, e), send_sem=b_send.at[0],
            recv_sem=b_recv.at[slot_of(dx, dz, e)], device_id={"sub": j}, device_id_type=MESH,
        ).wait_recv()

    for dz in (2, 1, -1, 0):
        for e in range(2):
            if dz or e:
                send_unit(
                    uq.at[core_of(e), lax.rem(z + dz % 4, 4)], qg.at[j, core], slot_of(0, -dz, e),
                    {"facet": 2 * y + core_of(e), "sub": place(0, dz)},
                )
    along_x(0, 0, 0, 1)
    along_x(0, 0, 0, -1)

    for copy in m_copies:
        copy.wait_recv()

    def column_phase(k):
        offset = jnp.zeros((1, 128), I32)
        for b in range(NS):
            offset = offset + jnp.where(meta_all[4 * x + k, 1:2, :] == b, meta_all[b, 0:1, :], 0)
        step = offset + 2044
        rows128 = iota((16, 128), 0)
        base_c, base_s = turn(((step * rows128) & (NIMG - 1)).astype(F32) * (1.0 / NIMG))
        for part in range(4):
            coarse_c, coarse_s = turn(((step * (16 * (rows128 + 16 * part))) & (NIMG - 1)).astype(F32) * (1.0 / NIMG))
            for q in range(16):
                cc, cs = coarse_c[q : q + 1], coarse_s[q : q + 1]
                at = part * 256 + q * 16
                ec[k, at : at + 16] = base_c * cc - base_s * cs
                es[k, at : at + 16] = -(base_s * cc + base_c * cs)

    def column_basis(k):
        half_steps(pos_all[4 * x + k, 1:2, :], ROWS, small)
        table_into(vb, (k,), BF16)

    def row_quarter(k):
        half_steps(pos_all[4 * x + k, 0:1, :], ROWS, small, 128.0 * lax.rem(z, 2).astype(F32))

        def put(at, lane_at, width, c, s):
            ub[k, pl.ds(at, 16), pl.ds(lane_at, width)] = jnp.where(z < 2, c, s)

        basis_into(small, lanes4, put, 8)

    def from_line(dz, e):
        arrived(0, dz, e)
        along_x(0, dz, e, 1)
        along_x(0, dz, e, -1)

    def across(dz):
        for e in range(2):
            for dx in (-1, 1):
                arrived(dx, dz, e)
                if e == (0 if dx == -1 else 1):
                    along_x(dx, dz, e, -dx)

    def transform(dx):
        line = lax.rem(x + dx % 4, 4)

        def modulate(i, carry):
            zz, cc = i // 2, lax.rem(i, 2)
            src = 4 * line + zz
            at = pl.multiple_of(src * 64 + cc * 32, 32)
            to = pl.multiple_of(i * 32, 32)
            re = qg[src, cc, :, 0:128].astype(F32)
            im = qg[src, cc, :, 128:256].astype(F32)
            for k in range(4):
                c, s = ec[k, pl.ds(at, 32)], es[k, pl.ds(at, 32)]
                qm[pl.ds(to, 32), k * 256 : k * 256 + 128] = (re * c - im * s).astype(BF16)
                qm[pl.ds(to, 32), k * 256 + 128 : k * 256 + 256] = (re * s + im * c).astype(BF16)
            return carry

        lax.fori_loop(0, 8, modulate, 0)
        lanes = pl.ds(pl.multiple_of(line * 256, 256), 256)
        for k in range(4):
            part = jnp.dot(bt[:, lanes], qm[:, k * 256 : k * 256 + 256], preferred_element_type=F32)
            if dx == 0:
                hacc[k] = part
            elif dx == 2:
                hs[k] = (hacc[k] + part).T.astype(BF16)
            else:
                hacc[k] += part

    column_phase(0)
    from_line(0, 1)
    column_phase(1)
    for dz in (-1, 1):
        for e in range(2):
            from_line(dz, e)
    column_phase(2)
    for e in range(2):
        from_line(2, e)
    column_phase(3)
    across(0)
    transform(0)
    column_basis(0)
    across(-1)
    column_basis(1)
    across(1)
    column_basis(2)
    across(2)
    column_basis(3)
    transform(-1)
    transform(1)
    for k in range(4):
        row_quarter(k)
    for dz in (0, -1, 1, 2):
        for e in range(2):
            arrived(2, dz, e)
    transform(2)

    part_copies = []
    for dz in (2, 1, -1, 0):
        k = lax.rem(z + dz % 4, 4)
        for at in range(0, ROWS, 256):
            lifted = jnp.dot(hs[k], vb[k, :, at : at + 256], preferred_element_type=F32)
            u = ub[k, :, at : at + 256]
            part_out[dz % 4, 0:1, at : at + 256] = jnp.sum(lifted[0:128] * u, axis=0, keepdims=True)
            part_out[dz % 4, 1:2, at : at + 256] = jnp.sum(lifted[128:256] * u, axis=0, keepdims=True)
        if dz:
            copy = pltpu.make_async_remote_copy(
                src_ref=part_out.at[dz % 4], dst_ref=part_in.at[-dz % 4],
                send_sem=d_send.at[dz % 4], recv_sem=d_recv.at[-dz % 4],
                device_id={"sub": place(0, dz)}, device_id_type=MESH,
            )
            copy.start()
            part_copies.append(copy)
    for copy in part_copies:
        copy.wait_recv()

    live_count = count[0]

    sums = part_out[0] + part_in[1] + part_in[2] + part_in[3]
    sum_re, sum_im = sums[0:1], sums[1:2]
    c, s = turn((pos[0, 0:1, :] + pos[0, 1:2, :]) * 0.5)
    scale = 4.0 / (M * FS)
    live = iota((1, ROWS), 1) < live_count
    re = obs[0, 0:1, :] - (sum_re * c + sum_im * s) * scale
    im = obs[0, 1:2, :] - (sum_im * c - sum_re * s) * scale
    both = jnp.concatenate([jnp.where(live, re, 0.0), jnp.where(live, im, 0.0)], axis=0)
    res_out[0] = both
    res_src[...] = both.astype(BF16)

    c_copies = []
    for d in range(1, NS):
        copy = pltpu.make_async_remote_copy(
            src_ref=res_src, dst_ref=res_all.at[j], send_sem=c_send.at[d - 1], recv_sem=c_recv.at[d - 1],
            device_id={"sub": lax.rem(j + d, NS)}, device_id_type=MESH,
        )
        copy.start()
        c_copies.append(copy)
    res_all[j] = res_src[...]

    rank = jnp.zeros((1, 128), F32)
    slots = [jnp.zeros((2, ROWS), F32) for _ in range(2)]
    for b in range(NS):
        match = jnp.where(meta_all[b, 1:2, :] == j, 1.0, 0.0)
        for slot in range(2):
            picked = jnp.where(rank == float(slot), match, 0.0)
            mask[slot, b : b + 1, :] = picked
            slots[slot] = slots[slot] + picked[:, 0:1] * pos_all[b]
        rank = rank + match
    for slot in range(2):
        slot_pos[slot] = slots[slot]
    for slot in range(2):
        half_steps(slot_pos[slot, 0:1, :], ROWS, small)
        table_into(ubo, (slot,), BF16)
        half_steps(slot_pos[slot, 1:2, :], ROWS, small)
        table_into(vbo, (slot,), F32)

    for copy in a_copies + m_copies + b_copies + part_copies:
        copy.wait_send()
    for copy in c_copies:
        copy.wait()

    rows = []
    for slot in range(2):
        r = jnp.zeros((2, ROWS), F32)
        for b in range(NS):
            r = r + mask[slot, b : b + 1, 0:1] * res_all[b].astype(F32)
        p = slot_pos[slot]
        c, s = turn((p[0:1, :] + p[1:2, :]) * 0.5)
        rows.append((r[0:1, :] * c - r[1:2, :] * s, r[0:1, :] * s + r[1:2, :] * c))
    for block in range(4):
        im, sine = block // 2, block % 2
        for slot in range(2):
            wb[block, :, slot * ROWS : slot * ROWS + ROWS] = (
                vbo[slot, sine * HALF : sine * HALF + HALF, :] * rows[slot][im]
            ).astype(BF16)
        for k in range(2):
            total[k, block] = sum(
                lax.dot_general(
                    ubo[slot, k * HALF : k * HALF + HALF, :], wb[block, :, slot * ROWS : slot * ROWS + ROWS],
                    (((1,), (1,)), ((), ())), preferred_element_type=F32,
                )
                for slot in range(2)
            )

    scale = 1.0 / math.sqrt(ROWS)
    flip = jnp.where(iota((HALF, HALF), 0) + iota((HALF, HALF), 1) == HALF - 1, 1.0, 0.0).astype(BF16)

    def flip_columns(a):
        return jnp.dot(a.astype(BF16), flip, preferred_element_type=F32).astype(BF16)

    def flip_rows(a):
        return jnp.dot(flip, a, preferred_element_type=F32).astype(BF16)

    for im in range(2):
        sign = 1.0 if im == 0 else -1.0
        cc, ss = total[0, 2 * im], total[1, 2 * im + 1]
        cs, sc = total[0, 3 - 2 * im], total[1, 2 - 2 * im]
        even, both = (cc - ss) * scale, (cc + ss) * scale
        y, w = (cs + sc) * (scale * sign), (cs - sc) * (scale * sign)
        left, right = slice(im * M, im * M + HALF), slice(im * M + HALF, im * M + M)
        grid_out[0, 0, HALF:M, right] = (even + y).astype(BF16)
        grid_out[0, 0, HALF:M, left] = flip_columns(both - w)
        grid_out[0, 0, 0:HALF, right] = flip_rows((both + w).astype(BF16))
        grid_out[0, 0, 0:HALF, left] = flip_rows(flip_columns(even - y))


def widen(res_in, grid_in, res_out, grid_out):
    res_out[...] = res_in[...]
    grid_out[...] = grid_in[...].astype(F32)


def per_device(facets, tapers, row_offsets, col_offsets, block_subgrid, vis_count, positions, observed):
    vmem = pl.BlockSpec(memory_space=pltpu.VMEM)
    dma = pltpu.SemaphoreType.DMA
    residual, grid = pl.pallas_call(
        front,
        out_shape=(
            jax.ShapeDtypeStruct((1, 2, ROWS), F32),
            jax.ShapeDtypeStruct((1, 1, M, 2 * M), BF16),
        ),
        in_specs=[pl.BlockSpec(memory_space=pltpu.HBM)] * 8,
        out_specs=(vmem, vmem),
        scratch_shapes=[
            pltpu.VMEM((2, FS), F32),
            pltpu.VMEM((1, 2, ROWS), F32),
            pltpu.VMEM((1, 2, ROWS), F32),
            pltpu.SMEM((NF,), I32),
            pltpu.SMEM((1,), I32),
            pltpu.SMEM((1, 1), I32),
            pltpu.SMEM((1,), I32),
            pltpu.VMEM((2, ROWS), BF16),
            pltpu.VMEM((NS, 2, ROWS), BF16),
            pltpu.VMEM((NS, 2, ROWS), F32),
            pltpu.VMEM((NS, 8, 128), I32),
            pltpu.VMEM((FS, 128), BF16),
            pltpu.VMEM((4, 32, FS), BF16),
            pltpu.VMEM((NF, 32, FS), BF16),
            pltpu.VMEM((M, FS), BF16),
            pltpu.VMEM((128, FS), BF16),
            pltpu.VMEM((2, 4, 32, 256), BF16),
            pltpu.VMEM((NS, 2, 32, 256), BF16),
            pltpu.VMEM((256, 1024), BF16),
            pltpu.VMEM((4, FS, 128), F32),
            pltpu.VMEM((4, FS, 128), F32),
            pltpu.VMEM((4, 128, ROWS), F32),
            pltpu.VMEM((4, M, ROWS), BF16),
            pltpu.VMEM((4, 256, M), BF16),
            pltpu.VMEM((4, M, 256), F32),
            pltpu.VMEM((4, 16, FS), F32),
            pltpu.VMEM((8, 128), I32),
            pltpu.VMEM((2, NS, 128), F32),
            pltpu.VMEM((2, 2, ROWS), F32),
            pltpu.VMEM((2, M, ROWS), BF16),
            pltpu.VMEM((2, M, ROWS), F32),
            pltpu.VMEM((4, HALF, 2 * ROWS), BF16),
            pltpu.VMEM((2, 4, HALF, HALF), F32),
            pltpu.VMEM((4, 2, ROWS), F32),
            pltpu.VMEM((4, 2, ROWS), F32),
            dma((8,)),
            dma((NF - 1,)), dma((8,)),
            dma((4,)), dma((4,)),
            dma((32,)), dma((32,)),
            dma((NS - 1,)), dma((NS - 1,)),
            dma((NS - 1,)), dma((NS - 1,)),
            dma((NS - 1,)), dma((NS - 1,)),
        ],
        compiler_params=pltpu.CompilerParams(collective_id=0, has_side_effects=True),
        name="front",
    )(facets, tapers, row_offsets, col_offsets, block_subgrid, vis_count, positions, observed)
    return pl.pallas_call(
        widen,
        out_shape=(
            jax.ShapeDtypeStruct((1, 2, ROWS), F32),
            jax.ShapeDtypeStruct((1, 1, M, 2 * M), F32),
        ),
        in_specs=[vmem, vmem],
        out_specs=(vmem, vmem),
        name="widen",
    )(residual, grid)


def solution(mesh):
    in_specs = (
        P("facet", None, None),
        P(),
        P(),
        P("sub"),
        P(("facet", "sub"), None),
        P(("facet", "sub")),
        P(("facet", "sub"), None, None),
        P(("facet", "sub"), None, None),
    )
    out_specs = (P(("facet", "sub"), None, None), P("facet", "sub", None, None))
    return jax.shard_map(per_device, mesh=mesh, in_specs=in_specs, out_specs=out_specs, check_vma=False)
```

time: 53.4 us -> 49.1 us (0.919)
  other arithmetic: 2.79 us -> 0 us
  Pallas kernels: 47.2 us -> 46.3 us
  local copies, waits for them, and re-layouts: 0.6 us -> 0 us
    pallas_call x1, Pallas kernels: 47.2 us -> 43.6 us  [per_device(): pl.pallas_call(front, out_shape=(jax.ShapeDtypeStruct((1, 2, ROWS), F32),...]
    convert_element_type x1 -> x0, other arithmetic: 2.79 us -> none  [per_device(): return (residual, grid.astype(F32))]
    pallas_call x0 -> x1, Pallas kernels: none -> 2.7 us  [per_device(): pl.pallas_call(widen, out_shape=(jax.ShapeDtypeStruct((1, 2, ROWS), F32),...]
    unnamed x3 -> x0, local copies, waits for them, and re-layouts: 0.6 us -> none
where the time goes in v1:
time: 49.1 us; the launch traced here: 48.9 us
  Pallas kernels  46.3 us (94%)
  between operations  2.58 us (5%)
    pallas_call x1, Pallas kernels, per_device(): pl.pallas_call(front, out_shape=(jax.ShapeDtypeStruct((1, 2, ROWS), F32),...  43.6 us
    pallas_call x1, Pallas kernels, per_device(): pl.pallas_call(widen, out_shape=(jax.ShapeDtypeStruct((1, 2, ROWS), F32),...  2.7 us

profile of v1, /device:TPU:0, one launch (start us, length us, event | category | flops | bytes accessed | tf_op | source)
XLA Modules:
  0.0 48.9 jit_solution(5135784452514187756)
XLA Ops:
  2.6 43.6 %front.1 = (f32[1,2,1024]{2,1,0:T(2,128)}, bf16[1,1,512,1024]{3,2,1,0:T(8,128)(2,1)}) custom-call(bf16[1,1024,1024]{2,1,0:T(8,128)(2,1)} %facets.1, f32[2,1024]{1,0:T(2,128)} %taper_in.1, s32[8]{0:T(128)} %row_off_in.1, s32[1]{0:T(128)S(6)} %copy.10.col_off_in, s32[1,1]{1,0:T(1,128)S(6)} %copy.11.target_in, s32[1]{0:T(128)S(6)} %copy.12.count_in, ...), custom_call_target="tpu_custom_call" | custom-call | tf_op jit(solution)/shard_map/front/pallas_call | solution.py:465
  46.2 2.7 %widen.1 = (f32[1,2,1024]{2,1,0:T(2,128)}, f32[1,1,512,1024]{3,2,1,0:T(8,128)}) custom-call(f32[1,2,1024]{2,1,0:T(2,128)} %get-tuple-element.4.res_in, bf16[1,1,512,1024]{3,2,1,0:T(8,128)(2,1)} %get-tuple-element.5.grid_in), custom_call_target="tpu_custom_call" | custom-call | tf_op jit(solution)/shard_map/widen/pallas_call | solution.py:520

commit v2 on v1

--- a/solution.py
+++ b/solution.py
@@ -436,10 +436,10 @@
     flip = jnp.where(iota((HALF, HALF), 0) + iota((HALF, HALF), 1) == HALF - 1, 1.0, 0.0).astype(BF16)
 
     def flip_columns(a):
-        return jnp.dot(a.astype(BF16), flip, preferred_element_type=F32).astype(BF16)
+        return jnp.dot(a.astype(BF16), flip, preferred_element_type=F32)
 
     def flip_rows(a):
-        return jnp.dot(flip, a, preferred_element_type=F32).astype(BF16)
+        return jnp.dot(flip, a, preferred_element_type=F32)
 
     for im in range(2):
         sign = 1.0 if im == 0 else -1.0
@@ -448,15 +448,21 @@
         even, both = (cc - ss) * scale, (cc + ss) * scale
         y, w = (cs + sc) * (scale * sign), (cs - sc) * (scale * sign)
         left, right = slice(im * M, im * M + HALF), slice(im * M + HALF, im * M + M)
-        grid_out[0, 0, HALF:M, right] = (even + y).astype(BF16)
+        grid_out[0, 0, HALF:M, right] = even + y
         grid_out[0, 0, HALF:M, left] = flip_columns(both - w)
         grid_out[0, 0, 0:HALF, right] = flip_rows((both + w).astype(BF16))
-        grid_out[0, 0, 0:HALF, left] = flip_rows(flip_columns(even - y))
-
-
-def widen(res_in, grid_in, res_out, grid_out):
-    res_out[...] = res_in[...]
-    grid_out[...] = grid_in[...].astype(F32)
+        grid_out[0, 0, 0:HALF, left] = flip_rows(flip_columns(even - y).astype(BF16))
+
+
+def store(res_in, grid_in, res_out, grid_out, sem):
+    copies = [
+        pltpu.make_async_copy(res_in, res_out, sem.at[0]),
+        pltpu.make_async_copy(grid_in, grid_out, sem.at[1]),
+    ]
+    for copy in copies:
+        copy.start()
+    for copy in copies:
+        copy.wait()
 
 
 def per_device(facets, tapers, row_offsets, col_offsets, block_subgrid, vis_count, positions, observed):
@@ -465,8 +471,8 @@
     residual, grid = pl.pallas_call(
         front,
         out_shape=(
-            jax.ShapeDtypeStruct((1, 2, ROWS), F32),
-            jax.ShapeDtypeStruct((1, 1, M, 2 * M), BF16),
+            pltpu.VMEM((1, 2, ROWS), F32),
+            pltpu.VMEM((1, 1, M, 2 * M), F32),
         ),
         in_specs=[pl.BlockSpec(memory_space=pltpu.HBM)] * 8,
         out_specs=(vmem, vmem),
@@ -517,16 +523,18 @@
         compiler_params=pltpu.CompilerParams(collective_id=0, has_side_effects=True),
         name="front",
     )(facets, tapers, row_offsets, col_offsets, block_subgrid, vis_count, positions, observed)
+    hbm = pl.BlockSpec(memory_space=pltpu.HBM)
     return pl.pallas_call(
-        widen,
+        store,
         out_shape=(
             jax.ShapeDtypeStruct((1, 2, ROWS), F32),
             jax.ShapeDtypeStruct((1, 1, M, 2 * M), F32),
         ),
         in_specs=[vmem, vmem],
-        out_specs=(vmem, vmem),
+        out_specs=(hbm, hbm),
+        scratch_shapes=[pltpu.SemaphoreType.DMA((2,))],
         name="widen",
-    )(residual, grid)
+    )(pltpu.with_memory_space_constraint(residual, pltpu.VMEM), pltpu.with_memory_space_constraint(grid, pltpu.VMEM))
 
 
 def solution(mesh):

time: 49.1 us -> 46.7 us (0.951)
  Pallas kernels: 46.3 us -> 44 us
    pallas_call x2, Pallas kernels: 46.3 us -> 44 us  [the longest x1 42.6 us: per_device(): pl.pallas_call(front, out_shape=(pltpu.VMEM((1, 2, ROWS), F32), pltpu.VME...]
where the time goes in v2:
time: 46.7 us; the launch traced here: 46.6 us
  Pallas kernels  44 us (94%)
  between operations  2.58 us (6%)
    pallas_call x1, Pallas kernels, per_device(): pl.pallas_call(front, out_shape=(pltpu.VMEM((1, 2, ROWS), F32), pltpu.VME...  42.6 us
    pallas_call x1, Pallas kernels, per_device(): pl.pallas_call(store, out_shape=(jax.ShapeDtypeStruct((1, 2, ROWS), F32),...  1.34 us

profile of v2, /device:TPU:0, one launch (start us, length us, event | category | flops | bytes accessed | tf_op | source)
XLA Modules:
  0.0 46.6 jit_solution(2556970103659091675)
XLA Ops:
  2.6 42.6 %front.1 = (f32[1,2,1024]{2,1,0:T(2,128)S(1)}, f32[1,1,512,1024]{3,2,1,0:T(8,128)S(1)}) custom-call(bf16[1,1024,1024]{2,1,0:T(8,128)(2,1)} %facets.1, f32[2,1024]{1,0:T(2,128)} %taper_in.1, s32[8]{0:T(128)} %row_off_in.1, s32[1]{0:T(128)S(6)} %copy.10.col_off_in, s32[1,1]{1,0:T(1,128)S(6)} %copy.11.target_in, s32[1]{0:T(128)S(6)} %copy.12.count_in, ...), custom_call_target="tpu_custom_call" | custom-call | tf_op jit(solution)/shard_map/front/pallas_call | solution.py:471
  45.2 1.3 %widen.1 = (f32[1,2,1024]{2,1,0:T(2,128)}, f32[1,1,512,1024]{3,2,1,0:T(8,128)}) custom-call(f32[1,2,1024]{2,1,0:T(2,128)S(1)} %get-tuple-element.4.res_in, f32[1,1,512,1024]{3,2,1,0:T(8,128)S(1)} %get-tuple-element.5.grid_in), custom_call_target="tpu_custom_call" | custom-call | tf_op jit(solution)/shard_map/widen/pallas_call | solution.py:527

commit v3 on v2

--- a/solution.py
+++ b/solution.py
@@ -123,24 +123,29 @@
     def facet_at(dy, c):
         return 2 * lax.rem(y + dy % 4, 4) + c
 
-    def send_slice(src, source, dy, c, slot):
+    def send_slice(src, source, dy, c, slot, h):
+        at = pl.ds(16 * h, 16)
         copy = pltpu.make_async_remote_copy(
-            src_ref=src, dst_ref=facs.at[source], send_sem=a_send.at[len(a_copies)], recv_sem=a_recv.at[slot],
+            src_ref=src.at[at], dst_ref=facs.at[source, at],
+            send_sem=a_send.at[len(a_copies)], recv_sem=a_recv.at[slot, h],
             device_id={"facet": facet_at(dy, c)}, device_id_type=MESH,
         )
         copy.start()
         a_copies.append(copy)
 
-    def slice_arrived(dy, c, slot):
+    def slice_arrived(dy, c, slot, h):
+        ref = facs.at[facet_at(dy, c), pl.ds(16 * h, 16)]
         pltpu.make_async_remote_copy(
-            src_ref=facs.at[facet_at(dy, c)], dst_ref=facs.at[facet_at(dy, c)],
-            send_sem=a_send.at[0], recv_sem=a_recv.at[slot], device_id={"facet": f}, device_id_type=MESH,
+            src_ref=ref, dst_ref=ref, send_sem=a_send.at[0], recv_sem=a_recv.at[slot, h],
+            device_id={"facet": f}, device_id_type=MESH,
         ).wait_recv()
 
-    for dy in (1, 3):
-        for c in range(2):
-            send_slice(tt.at[2 * odd + c], f, dy, c, 2 * (4 - dy) + core)
-    send_slice(tt.at[2 * odd + 1 - core], f, 0, 1 - core, 0)
+    for h in range(2):
+        for dy in (1, 3):
+            for c in range(2):
+                send_slice(tt.at[2 * odd + c], f, dy, c, 2 * (4 - dy) + core, h)
+    for h in range(2):
+        send_slice(tt.at[2 * odd + 1 - core], f, 0, 1 - core, 0, h)
     for d in range(1, NS):
         peer = lax.rem(j + d, NS)
         for src, dst, ss, rs in ((meta_src, meta_all, m_send, m_recv), (pos.at[0], pos_all, p_send, p_recv)):
@@ -161,17 +166,18 @@
         basis_into(small, lanes4, put)
 
     def relay_slices():
-        slice_arrived(3, 0, 6)
-        send_slice(facs.at[facet_at(3, 0)], facet_at(3, 0), 1, core, 4)
-        slice_arrived(1, 1, 3)
-        send_slice(facs.at[facet_at(1, 1)], facet_at(1, 1), 3, core, 5)
+        for h in range(2):
+            slice_arrived(3, 0, 6, h)
+            send_slice(facs.at[facet_at(3, 0)], facet_at(3, 0), 1, core, 4, h)
+            slice_arrived(1, 1, 3, h)
+            send_slice(facs.at[facet_at(1, 1)], facet_at(1, 1), 3, core, 5, h)
 
     lane = iota((16, FS), 1)
     row = iota((16, FS), 0)
     small[0], small[1] = turn((((2 * row + 1) * lane) & 2047).astype(F32) * (1.0 / 2048))
     small[2], small[3] = turn(((32 * row * lane) & 2047).astype(F32) * (1.0 / 2048))
+    relay_slices()
     table_into(bt, (), BF16)
-    relay_slices()
 
     phases = []
     rows_f = iota((NF, FS), 0)
@@ -182,11 +188,45 @@
         c, s = turn(r.astype(F32) * (1.0 / NIMG))
         phases.append((c, -s))
 
-    slice_arrived(0, 1 - core, 0)
-    slice_arrived(3, 1, 7)
-    slice_arrived(1, 0, 2)
-    slice_arrived(2, 0, 4)
-    slice_arrived(2, 1, 5)
+    def column_phase(k):
+        offset = jnp.zeros((1, 128), I32)
+        for b in range(NS):
+            offset = offset + jnp.where(meta_all[4 * x + k, 1:2, :] == b, meta_all[b, 0:1, :], 0)
+        step = offset + 2044
+        rows128 = iota((16, 128), 0)
+        base_c, base_s = turn(((step * rows128) & (NIMG - 1)).astype(F32) * (1.0 / NIMG))
+        for part in range(4):
+            coarse_c, coarse_s = turn(((step * (16 * (rows128 + 16 * part))) & (NIMG - 1)).astype(F32) * (1.0 / NIMG))
+            for q in range(16):
+                cc, cs = coarse_c[q : q + 1], coarse_s[q : q + 1]
+                at = part * 256 + q * 16
+                ec[k, at : at + 16] = base_c * cc - base_s * cs
+                es[k, at : at + 16] = -(base_s * cc + base_c * cs)
+
+    def column_basis(k):
+        half_steps(pos_all[4 * x + k, 1:2, :], ROWS, small)
+        table_into(vb, (k,), BF16)
+
+    def row_quarter(k):
+        half_steps(pos_all[4 * x + k, 0:1, :], ROWS, small, 128.0 * lax.rem(z, 2).astype(F32))
+
+        def put(at, lane_at, width, c, s):
+            ub[k, pl.ds(at, 16), pl.ds(lane_at, width)] = jnp.where(z < 2, c, s)
+
+        basis_into(small, lanes4, put, 8)
+
+    column_basis(z)
+    row_quarter(z)
+    def slot_table(slot, k):
+        half_steps(slot_pos[slot, k : k + 1, :], ROWS, small)
+        table_into(ubo if k == 0 else vbo, (slot,), BF16 if k == 0 else F32)
+
+    def other(i):
+        return lax.rem(z + i, 4)
+
+    for dy, c, slot in ((0, 1 - core, 0), (3, 1, 7), (1, 0, 2), (2, 0, 4), (2, 1, 5)):
+        for h in range(2):
+            slice_arrived(dy, c, slot, h)
     for at, width in lanes4:
         sums = [jnp.zeros((32, width), F32) for _ in range(4)]
         for g in range(NF):
@@ -251,32 +291,18 @@
     for copy in m_copies:
         copy.wait_recv()
 
-    def column_phase(k):
-        offset = jnp.zeros((1, 128), I32)
-        for b in range(NS):
-            offset = offset + jnp.where(meta_all[4 * x + k, 1:2, :] == b, meta_all[b, 0:1, :], 0)
-        step = offset + 2044
-        rows128 = iota((16, 128), 0)
-        base_c, base_s = turn(((step * rows128) & (NIMG - 1)).astype(F32) * (1.0 / NIMG))
-        for part in range(4):
-            coarse_c, coarse_s = turn(((step * (16 * (rows128 + 16 * part))) & (NIMG - 1)).astype(F32) * (1.0 / NIMG))
-            for q in range(16):
-                cc, cs = coarse_c[q : q + 1], coarse_s[q : q + 1]
-                at = part * 256 + q * 16
-                ec[k, at : at + 16] = base_c * cc - base_s * cs
-                es[k, at : at + 16] = -(base_s * cc + base_c * cs)
-
-    def column_basis(k):
-        half_steps(pos_all[4 * x + k, 1:2, :], ROWS, small)
-        table_into(vb, (k,), BF16)
-
-    def row_quarter(k):
-        half_steps(pos_all[4 * x + k, 0:1, :], ROWS, small, 128.0 * lax.rem(z, 2).astype(F32))
-
-        def put(at, lane_at, width, c, s):
-            ub[k, pl.ds(at, 16), pl.ds(lane_at, width)] = jnp.where(z < 2, c, s)
-
-        basis_into(small, lanes4, put, 8)
+    rank = jnp.zeros((1, 128), F32)
+    slots = [jnp.zeros((2, ROWS), F32) for _ in range(2)]
+    for b in range(NS):
+        match = jnp.where(meta_all[b, 1:2, :] == j, 1.0, 0.0)
+        for slot in range(2):
+            picked = jnp.where(rank == float(slot), match, 0.0)
+            mask[slot, b : b + 1, :] = picked
+            slots[slot] = slots[slot] + picked[:, 0:1] * pos_all[b]
+        rank = rank + match
+    for slot in range(2):
+        slot_pos[slot] = slots[slot]
+    column_phase(z)
 
     def from_line(dz, e):
         arrived(0, dz, e)
@@ -317,29 +343,28 @@
             else:
                 hacc[k] += part
 
-    column_phase(0)
     from_line(0, 1)
-    column_phase(1)
+    column_phase(other(1))
     for dz in (-1, 1):
         for e in range(2):
             from_line(dz, e)
-    column_phase(2)
+    column_phase(other(2))
     for e in range(2):
         from_line(2, e)
-    column_phase(3)
+    column_phase(other(3))
     across(0)
     transform(0)
-    column_basis(0)
+    column_basis(other(1))
     across(-1)
-    column_basis(1)
+    column_basis(other(2))
     across(1)
-    column_basis(2)
+    column_basis(other(3))
     across(2)
-    column_basis(3)
+    row_quarter(other(1))
     transform(-1)
     transform(1)
-    for k in range(4):
-        row_quarter(k)
+    row_quarter(other(2))
+    row_quarter(other(3))
     for dz in (0, -1, 1, 2):
         for e in range(2):
             arrived(2, dz, e)
@@ -387,22 +412,10 @@
         c_copies.append(copy)
     res_all[j] = res_src[...]
 
-    rank = jnp.zeros((1, 128), F32)
-    slots = [jnp.zeros((2, ROWS), F32) for _ in range(2)]
-    for b in range(NS):
-        match = jnp.where(meta_all[b, 1:2, :] == j, 1.0, 0.0)
-        for slot in range(2):
-            picked = jnp.where(rank == float(slot), match, 0.0)
-            mask[slot, b : b + 1, :] = picked
-            slots[slot] = slots[slot] + picked[:, 0:1] * pos_all[b]
-        rank = rank + match
-    for slot in range(2):
-        slot_pos[slot] = slots[slot]
-    for slot in range(2):
-        half_steps(slot_pos[slot, 0:1, :], ROWS, small)
-        table_into(ubo, (slot,), BF16)
-        half_steps(slot_pos[slot, 1:2, :], ROWS, small)
-        table_into(vbo, (slot,), F32)
+    slot_table(0, 0)
+    slot_table(0, 1)
+    slot_table(1, 0)
+    slot_table(1, 1)
 
     for copy in a_copies + m_copies + b_copies + part_copies:
         copy.wait_send()
@@ -423,14 +436,15 @@
             wb[block, :, slot * ROWS : slot * ROWS + ROWS] = (
                 vbo[slot, sine * HALF : sine * HALF + HALF, :] * rows[slot][im]
             ).astype(BF16)
-        for k in range(2):
-            total[k, block] = sum(
-                lax.dot_general(
-                    ubo[slot, k * HALF : k * HALF + HALF, :], wb[block, :, slot * ROWS : slot * ROWS + ROWS],
-                    (((1,), (1,)), ((), ())), preferred_element_type=F32,
-                )
-                for slot in range(2)
+        product = sum(
+            lax.dot_general(
+                ubo[slot], wb[block, :, slot * ROWS : slot * ROWS + ROWS],
+                (((1,), (1,)), ((), ())), preferred_element_type=F32,
             )
+            for slot in range(2)
+        )
+        total[0, block] = product[0:HALF]
+        total[1, block] = product[HALF:M]
 
     scale = 1.0 / math.sqrt(ROWS)
     flip = jnp.where(iota((HALF, HALF), 0) + iota((HALF, HALF), 1) == HALF - 1, 1.0, 0.0).astype(BF16)
@@ -513,7 +527,7 @@
             pltpu.VMEM((4, 2, ROWS), F32),
             pltpu.VMEM((4, 2, ROWS), F32),
             dma((8,)),
-            dma((NF - 1,)), dma((8,)),
+            dma((14,)), dma((8, 2)),
             dma((4,)), dma((4,)),
             dma((32,)), dma((32,)),
             dma((NS - 1,)), dma((NS - 1,)),

time: 46.7 us -> 46 us (0.985)
  Pallas kernels: 44 us -> 43.2 us
    pallas_call x1, Pallas kernels: 42.6 us -> 41.9 us  [per_device(): pl.pallas_call(front, out_shape=(pltpu.VMEM((1, 2, ROWS), F32), pltpu.VME...]
where the time goes in v3:
time: 46 us; the launch traced here: 45.8 us
  Pallas kernels  43.2 us (94%)
  between operations  2.58 us (6%)
    pallas_call x1, Pallas kernels, per_device(): pl.pallas_call(front, out_shape=(pltpu.VMEM((1, 2, ROWS), F32), pltpu.VME...  41.9 us
    pallas_call x1, Pallas kernels, per_device(): pl.pallas_call(store, out_shape=(jax.ShapeDtypeStruct((1, 2, ROWS), F32),...  1.34 us

profile of v3, /device:TPU:0, one launch (start us, length us, event | category | flops | bytes accessed | tf_op | source)
XLA Modules:
  0.0 45.8 jit_solution(8220043427280731037)
XLA Ops:
  2.6 41.9 %front.1 = (f32[1,2,1024]{2,1,0:T(2,128)S(1)}, f32[1,1,512,1024]{3,2,1,0:T(8,128)S(1)}) custom-call(bf16[1,1024,1024]{2,1,0:T(8,128)(2,1)} %facets.1, f32[2,1024]{1,0:T(2,128)} %taper_in.1, s32[8]{0:T(128)} %row_off_in.1, s32[1]{0:T(128)S(6)} %copy.10.col_off_in, s32[1,1]{1,0:T(1,128)S(6)} %copy.11.target_in, s32[1]{0:T(128)S(6)} %copy.12.count_in, ...), custom_call_target="tpu_custom_call" | custom-call | tf_op jit(solution)/shard_map/front/pallas_call | solution.py:485
  44.5 1.3 %widen.1 = (f32[1,2,1024]{2,1,0:T(2,128)}, f32[1,1,512,1024]{3,2,1,0:T(8,128)}) custom-call(f32[1,2,1024]{2,1,0:T(2,128)S(1)} %get-tuple-element.4.res_in, f32[1,1,512,1024]{3,2,1,0:T(8,128)S(1)} %get-tuple-element.5.grid_in), custom_call_target="tpu_custom_call" | custom-call | tf_op jit(solution)/shard_map/widen/pallas_call | solution.py:541
